TPU v7x, 32 devices: a whole 2x2x4 slice. The times are simulated.
32 devices in a mesh: blk: 4 (over z), grp: 8 (over y, x, core).
Axes of the slice: x: 2, y: 2, z: 4, core: 2. Of those that a mesh axis runs over, the one named last changes fastest.
Arguments:
- position: float32 [3, 16384], P(None, ('blk', 'grp')), may hold values from -6 to 6
- velocity: float32 [3, 16384], P(None, ('blk', 'grp')), may hold values from -6 to 6
- accel_old: float32 [3, 16384], P(None, ('blk', 'grp')), may hold values from -6 to 6
- jerk_old: float32 [3, 16384], P(None, ('blk', 'grp')), may hold values from -6 to 6
- mass: float32 [16384], P(('blk', 'grp')), may hold values from 1e-07 to 1e-05
- elapsed: float32 [16384], P(('blk', 'grp')), may hold values from 0.1 to 1
- active_index: int32 [512], P(('blk', 'grp')), may hold values from 0 to 16383, as said below
Outputs:
- predicted: float32 [6, 16384], P(None, ('blk', 'grp'))
- accel: float32 [3, 512], P(None, ('blk', 'grp'))
- jerk: float32 [3, 512], P(None, ('blk', 'grp'))
Inputs may be any that keep to these rules, and one draw needn't show every extreme that they name: `active_index`: entries 16 * k to 16 * k + 15 are distinct stars of the range 512 * k to 512 * k + 511, for every k.
All inputs are finite; a program needn't handle non-finite values.
Results may differ from a plain program's by a relative error of at most 0.0003.
Values sent between devices are 32-bit elements; how exact they have to be, the bound alone decides.
A program may use at most 64 MiB of HBM per device.

v0:
```python
import math

import jax
import jax.numpy as jnp
from jax import lax
from jax.sharding import PartitionSpec as P

SOFTENING = 0.0001


def from_behind(shard, axis, by):
    count = lax.axis_size(axis)
    return lax.ppermute(shard, axis, [(i, (i + by) % count) for i in range(count)])


def predict(position, velocity, accel_old, jerk_old, elapsed):
    step_row = elapsed[None, :]
    half = step_row * step_row * 0.5
    sixth = half * step_row * (1.0 / 3.0)
    new_position = position + step_row * velocity + half * accel_old + sixth * jerk_old
    new_velocity = velocity + step_row * accel_old + half * jerk_old
    return jnp.concatenate([new_position, new_velocity], 0)


def interact(targets, sources, masses):
    columns = targets.shape[1]
    block_size = math.gcd(columns, 128)
    blocks = columns // block_size
    stacked = targets.reshape(6, blocks, block_size).transpose(1, 0, 2)

    def one_block(target_block):
        separation = sources[0:3][:, None, :] - target_block[0:3][:, :, None]
        relative = sources[3:6][:, None, :] - target_block[3:6][:, :, None]
        distance = jnp.sum(separation * separation, 0) + SOFTENING
        inverse = 1.0 / jnp.sqrt(distance)
        weight = masses[None, :] * inverse * inverse * inverse
        radial = 3.0 * jnp.sum(separation * relative, 0) / distance
        accel_part = jnp.sum(weight[None] * separation, 2)
        jerk_part = jnp.sum(weight[None] * (relative - radial[None] * separation), 2)
        return jnp.concatenate([accel_part, jerk_part], 0)

    result = lax.map(one_block, stacked)
    return result.transpose(1, 0, 2).reshape(6, columns)


def local(position, velocity, accel_old, jerk_old, mass, elapsed, active_index):
    predicted = predict(position, velocity, accel_old, jerk_old, elapsed)
    stars_here = position.shape[1]
    device = lax.axis_index("blk") * lax.axis_size("grp") + lax.axis_index("grp")
    offsets = active_index - device * stars_here
    owned_rows = jnp.take(predicted, offsets, axis=1)
    group_rows = lax.all_gather(owned_rows, "grp", axis=1, tiled=True)

    def circulate(number, carry):
        visitor, partial_value = carry
        partial_value = partial_value + interact(visitor, predicted, mass)
        return from_behind((visitor, partial_value), "blk", 1)

    start = jnp.zeros(group_rows.shape, jnp.float32)
    visitor, partial_value = lax.fori_loop(0, lax.axis_size("blk"), circulate, (group_rows, start))
    owned = lax.psum_scatter(partial_value, "grp", scatter_dimension=1, tiled=True)
    return (predicted, owned[0:3], owned[3:6])


def solution(mesh):
    in_specs = (
        P(None, ("blk", "grp")),
        P(None, ("blk", "grp")),
        P(None, ("blk", "grp")),
        P(None, ("blk", "grp")),
        P(("blk", "grp")),
        P(("blk", "grp")),
        P(("blk", "grp")),
    )
    out_specs = (P(None, ("blk", "grp")), P(None, ("blk", "grp")), P(None, ("blk", "grp")))
    return jax.shard_map(local, mesh=mesh, in_specs=in_specs, out_specs=out_specs, check_vma=False)
```

profile of v0, /device:TPU:0, one launch (start us, length us, event | category | flops | bytes accessed | tf_op | source)
XLA Modules:
  0.0 89.8 jit_solution(8160792300937886255)
XLA Ops:
  7.3 0.6 copy-done.7
  7.9 0.7 copy-done.2
  8.8 0.4 copy-done
  9.3 0.6 gather_fusion
  10.0 10.6 %all-gather = f32[8,16,6]{1,2,0:T(8,128)S(1)} all-gather(f32[1,16,6]{1,2,0:T(8,128)S(1)} %bitcast.9), channel_id=1, replica_groups=mesh['blk'=4,'grp'=8] {'grp'}, dimensions={0}, use_global_device_ids=true | all-gather | bytes 3456 | tf_op jit(solution)/shard_map/all_gather | solution.py:52
  20.7 0.7 copy-done.1
  21.3 26.4 %while.11 = (s32[]{:T(128)}, f32[6,128]{1,0:T(8,128)S(1)}, f32[6,128]{1,0:T(8,128)S(1)}, f32[3,512]{1,0:T(4,128)S(1)}, f32[512]{0:T(512)S(1)}, /*index=5*/f32[3,512]{1,0:T(4,128)S(1)}, s32[]{:T(128)}) while((s32[]{:T(128)}, f32[6,128]{1,0:T(8,128)S(1)}, f32[6,128]{1,0:T(8,128)S(1)}, f32[3,512]{1,0:T(4,128)S(1)}, f32[512]{0:T(512)S(1)}, ...), condition=%wide.region_5.6_spmd, body=%wide.region_0.5_spmd.sunk | while | flops 3015426 | bytes 2179229 | solution.py:60
  21.3 1.6 %collective-permute-start = (f32[6,128]{1,0:T(8,128)S(1)}, f32[6,128]{1,0:T(8,128)S(1)}, u32[]{:S(2)}, u32[]{:S(2)}) collective-permute-start(f32[6,128]{1,0:T(8,128)S(1)} %copy.57), channel_id=1, source_target_pairs={{0,8},{8,16},{16,24},{24,0},{1,9},{9,17},{17,25},{25,1},{2,10},{10... | collective-permute-start | bytes 9224 | tf_op jit(solution)/shard_map/while/body/eval_jaxpr/ppermute | solution.py:13
  22.9 0.2 fusion.11
  23.2 0.4 fusion.12
  23.6 1.6 %collective-permute-start.1 = (f32[6,128]{1,0:T(8,128)S(1)}, f32[6,128]{1,0:T(8,128)S(1)}, u32[]{:S(2)}, u32[]{:S(2)}) collective-permute-start(f32[6,128]{1,0:T(8,128)S(1)} %maximum_add_fusion.2), channel_id=1, source_target_pairs={{0,8},{8,16},{16,24},{24,0},{1,9},{9,17},{17,25},{25,1},{2,10},{10... | collective-permute-start | bytes 9224 | tf_op jit(solution)/shard_map/while/body/eval_jaxpr/ppermute | solution.py:13
  25.3 1.5 %collective-permute-done = f32[6,128]{1,0:T(8,128)S(1)} collective-permute-done((f32[6,128]{1,0:T(8,128)S(1)}, f32[6,128]{1,0:T(8,128)S(1)}, u32[]{:S(2)}, u32[]{:S(2)}) %collective-permute-start) | collective-permute-done | bytes 3104 | tf_op jit(solution)/shard_map/while/body/eval_jaxpr/ppermute | solution.py:13
  26.7 2.4 %collective-permute-done.1 = f32[6,128]{1,0:T(8,128)S(1)} collective-permute-done((f32[6,128]{1,0:T(8,128)S(1)}, f32[6,128]{1,0:T(8,128)S(1)}, u32[]{:S(2)}, u32[]{:S(2)}) %collective-permute-start.1) | collective-permute-done | bytes 3104 | tf_op jit(solution)/shard_map/while/body/eval_jaxpr/ppermute | solution.py:13
  29.1 0.2 fusion.11
  29.4 0.4 fusion.12
  29.8 1.4 %collective-permute-start.1 = (f32[6,128]{1,0:T(8,128)S(1)}, f32[6,128]{1,0:T(8,128)S(1)}, u32[]{:S(2)}, u32[]{:S(2)}) collective-permute-start(f32[6,128]{1,0:T(8,128)S(1)} %maximum_add_fusion.2), channel_id=1, source_target_pairs={{0,8},{8,16},{16,24},{24,0},{1,9},{9,17},{17,25},{25,1},{2,10},{10... | collective-permute-start | bytes 9224 | tf_op jit(solution)/shard_map/while/body/eval_jaxpr/ppermute | solution.py:13
  31.2 3.3 %collective-permute-done = f32[6,128]{1,0:T(8,128)S(1)} collective-permute-done((f32[6,128]{1,0:T(8,128)S(1)}, f32[6,128]{1,0:T(8,128)S(1)}, u32[]{:S(2)}, u32[]{:S(2)}) %collective-permute-start) | collective-permute-done | bytes 3104 | tf_op jit(solution)/shard_map/while/body/eval_jaxpr/ppermute | solution.py:13
  34.5 0.8 collective-permute-done.1
  35.3 0.2 fusion.11
  35.6 0.4 fusion.12
  36.0 0.9 %collective-permute-start.1 = (f32[6,128]{1,0:T(8,128)S(1)}, f32[6,128]{1,0:T(8,128)S(1)}, u32[]{:S(2)}, u32[]{:S(2)}) collective-permute-start(f32[6,128]{1,0:T(8,128)S(1)} %maximum_add_fusion.2), channel_id=1, source_target_pairs={{0,8},{8,16},{16,24},{24,0},{1,9},{9,17},{17,25},{25,1},{2,10},{10... | collective-permute-start | bytes 9224 | tf_op jit(solution)/shard_map/while/body/eval_jaxpr/ppermute | solution.py:13
  37.0 3.8 %collective-permute-done = f32[6,128]{1,0:T(8,128)S(1)} collective-permute-done((f32[6,128]{1,0:T(8,128)S(1)}, f32[6,128]{1,0:T(8,128)S(1)}, u32[]{:S(2)}, u32[]{:S(2)}) %collective-permute-start) | collective-permute-done | bytes 3104 | tf_op jit(solution)/shard_map/while/body/eval_jaxpr/ppermute | solution.py:13
  40.7 0.8 collective-permute-done.1
  41.8 0.4 fusion.12
  42.2 1.4 %collective-permute-start.1 = (f32[6,128]{1,0:T(8,128)S(1)}, f32[6,128]{1,0:T(8,128)S(1)}, u32[]{:S(2)}, u32[]{:S(2)}) collective-permute-start(f32[6,128]{1,0:T(8,128)S(1)} %maximum_add_fusion.2), channel_id=1, source_target_pairs={{0,8},{8,16},{16,24},{24,0},{1,9},{9,17},{17,25},{25,1},{2,10},{10... | collective-permute-start | bytes 9224 | tf_op jit(solution)/shard_map/while/body/eval_jaxpr/ppermute | solution.py:13
  43.6 3.3 %collective-permute-done = f32[6,128]{1,0:T(8,128)S(1)} collective-permute-done((f32[6,128]{1,0:T(8,128)S(1)}, f32[6,128]{1,0:T(8,128)S(1)}, u32[]{:S(2)}, u32[]{:S(2)}) %collective-permute-start) | collective-permute-done | bytes 3104 | tf_op jit(solution)/shard_map/while/body/eval_jaxpr/ppermute | solution.py:13
  46.9 0.8 collective-permute-done.1
  47.7 0.7 copy.49
  48.5 32.4 %reduce-scatter.4.cloned.1.call-done = f32[16,6]{1,0:T(8,128)} async-done(((f32[128,6]{1,0:T(8,128)}), f32[16,6]{1,0:T(8,128)}) %reduce-scatter.4.cloned.1.call-update) | async-done | bytes 400
  80.8 0.8 fusion.6
  81.7 0.7 copy.52
  82.3 0.7 copy.51
  (45 shorter events, 1.1 us)
Async XLA Ops:
  7.2 73.7 %reduce-scatter.4.cloned.1.call-start = ((), (), s32[]{:S(2)}) async-start(), calls=%async_computation.1 | async-start | bytes 73728
  7.2 1.4 %copy-start.6 = (f32[3,512]{1,0:T(4,128)S(1)}, f32[3,512]{1,0:T(4,128)}, u32[]{:S(2)}) copy-start(f32[3,512]{1,0:T(4,128)} %param.10) | copy-start | bytes 18436
  7.2 1.4 %copy-start.5 = (f32[3,512]{1,0:T(4,128)S(1)}, f32[3,512]{1,0:T(4,128)}, u32[]{:S(2)}) copy-start(f32[3,512]{1,0:T(4,128)} %param.9) | copy-start | bytes 18436
  7.2 0.7 copy-start.7
  7.2 1.4 %copy-start.4 = (f32[3,512]{1,0:T(4,128)S(1)}, f32[3,512]{1,0:T(4,128)}, u32[]{:S(2)}) copy-start(f32[3,512]{1,0:T(4,128)} %param.11) | copy-start | bytes 18436
  7.9 0.7 copy-start.2
  7.9 0.7 copy-start.3
  8.7 0.6 copy-start
  20.7 0.7 copy-start.1
  21.3 5.4 %collective-permute-start = (f32[6,128]{1,0:T(8,128)S(1)}, f32[6,128]{1,0:T(8,128)S(1)}, u32[]{:S(2)}, u32[]{:S(2)}) collective-permute-start(f32[6,128]{1,0:T(8,128)S(1)} %copy.57), channel_id=1, source_target_pairs={{0,8},{8,16},{16,24},{24,0},{1,9},{9,17},{17,25},{25,1},{2,10},{10... | collective-permute-start | bytes 9224 | tf_op jit(solution)/shard_map/while/body/eval_jaxpr/ppermute | solution.py:13
  23.6 5.5 %collective-permute-start.1 = (f32[6,128]{1,0:T(8,128)S(1)}, f32[6,128]{1,0:T(8,128)S(1)}, u32[]{:S(2)}, u32[]{:S(2)}) collective-permute-start(f32[6,128]{1,0:T(8,128)S(1)} %maximum_add_fusion.2), channel_id=1, source_target_pairs={{0,8},{8,16},{16,24},{24,0},{1,9},{9,17},{17,25},{25,1},{2,10},{10... | collective-permute-start | bytes 9224 | tf_op jit(solution)/shard_map/while/body/eval_jaxpr/ppermute | solution.py:13
  29.1 5.4 %collective-permute-start = (f32[6,128]{1,0:T(8,128)S(1)}, f32[6,128]{1,0:T(8,128)S(1)}, u32[]{:S(2)}, u32[]{:S(2)}) collective-permute-start(f32[6,128]{1,0:T(8,128)S(1)} %copy.57), channel_id=1, source_target_pairs={{0,8},{8,16},{16,24},{24,0},{1,9},{9,17},{17,25},{25,1},{2,10},{10... | collective-permute-start | bytes 9224 | tf_op jit(solution)/shard_map/while/body/eval_jaxpr/ppermute | solution.py:13
  29.8 5.5 %collective-permute-start.1 = (f32[6,128]{1,0:T(8,128)S(1)}, f32[6,128]{1,0:T(8,128)S(1)}, u32[]{:S(2)}, u32[]{:S(2)}) collective-permute-start(f32[6,128]{1,0:T(8,128)S(1)} %maximum_add_fusion.2), channel_id=1, source_target_pairs={{0,8},{8,16},{16,24},{24,0},{1,9},{9,17},{17,25},{25,1},{2,10},{10... | collective-permute-start | bytes 9224 | tf_op jit(solution)/shard_map/while/body/eval_jaxpr/ppermute | solution.py:13
  35.3 5.4 %collective-permute-start = (f32[6,128]{1,0:T(8,128)S(1)}, f32[6,128]{1,0:T(8,128)S(1)}, u32[]{:S(2)}, u32[]{:S(2)}) collective-permute-start(f32[6,128]{1,0:T(8,128)S(1)} %copy.57), channel_id=1, source_target_pairs={{0,8},{8,16},{16,24},{24,0},{1,9},{9,17},{17,25},{25,1},{2,10},{10... | collective-permute-start | bytes 9224 | tf_op jit(solution)/shard_map/while/body/eval_jaxpr/ppermute | solution.py:13
  36.0 5.5 %collective-permute-start.1 = (f32[6,128]{1,0:T(8,128)S(1)}, f32[6,128]{1,0:T(8,128)S(1)}, u32[]{:S(2)}, u32[]{:S(2)}) collective-permute-start(f32[6,128]{1,0:T(8,128)S(1)} %maximum_add_fusion.2), channel_id=1, source_target_pairs={{0,8},{8,16},{16,24},{24,0},{1,9},{9,17},{17,25},{25,1},{2,10},{10... | collective-permute-start | bytes 9224 | tf_op jit(solution)/shard_map/while/body/eval_jaxpr/ppermute | solution.py:13
  41.5 5.4 %collective-permute-start = (f32[6,128]{1,0:T(8,128)S(1)}, f32[6,128]{1,0:T(8,128)S(1)}, u32[]{:S(2)}, u32[]{:S(2)}) collective-permute-start(f32[6,128]{1,0:T(8,128)S(1)} %copy.57), channel_id=1, source_target_pairs={{0,8},{8,16},{16,24},{24,0},{1,9},{9,17},{17,25},{25,1},{2,10},{10... | collective-permute-start | bytes 9224 | tf_op jit(solution)/shard_map/while/body/eval_jaxpr/ppermute | solution.py:13
  42.2 5.5 %collective-permute-start.1 = (f32[6,128]{1,0:T(8,128)S(1)}, f32[6,128]{1,0:T(8,128)S(1)}, u32[]{:S(2)}, u32[]{:S(2)}) collective-permute-start(f32[6,128]{1,0:T(8,128)S(1)} %maximum_add_fusion.2), channel_id=1, source_target_pairs={{0,8},{8,16},{16,24},{24,0},{1,9},{9,17},{17,25},{25,1},{2,10},{10... | collective-permute-start | bytes 9224 | tf_op jit(solution)/shard_map/while/body/eval_jaxpr/ppermute | solution.py:13
Sparse Core Ops, SparseCore 0:
  48.6 32.2 reduce-scatter.3
where the time goes:
time: 90.2 us; the launch traced here: 89.8 us
  waiting for transfers between devices  48.9 us (54%)
  between operations  14.1 us (16%)
  blocking collectives  10.6 us (12%)
  starting transfers between devices  6.96 us (8%)
  local copies, waits for them, and re-layouts  6.22 us (7%)
  other arithmetic  2.95 us (3%)
    unnamed x2, waiting for transfers between devices  32.4 us
    ppermute x8, waiting for transfers between devices, from_behind(): lax.ppermute(shard, axis, [(i, (i + by) % count) for i in range(count)])  16.5 us
    all_gather x1, blocking collectives, local(): group_rows = lax.all_gather(owned_rows, 'grp', axis=1, tiled=True)  10.6 us
    ppermute x8, starting transfers between devices, from_behind(): lax.ppermute(shard, axis, [(i, (i + by) % count) for i in range(count)])  6.93 us
    unnamed x20, local copies, waits for them, and re-layouts  4.56 us
  transfers between devices with their start and end apart: 9, of which 9 were waited for; matrix products, arithmetic and copies ran while one was open for 3% of the time, Pallas kernels for 0%

commit v1 on v0

v1 whole, which is shorter than its diff:
```python
import functools

import jax
import jax.numpy as jnp
from jax import lax
from jax.experimental import pallas as pl
from jax.experimental.pallas import tpu as pltpu
from jax.sharding import PartitionSpec as P

SOFTENING = 0.0001
LANES = 128
ROWS = 8


def flipped(index, mask):
    out, bit = index, 1
    while bit <= mask:
        if mask & bit:
            out = out + bit - 2 * bit * lax.rem(lax.div(index, bit), 2)
        bit *= 2
    return out


def kernel(
    n_blk, n_grp, stars, active,
    position, velocity, accel_old, jerk_old, mass, elapsed, index,
    predicted, accel, jerk,
    in_pos, in_vel, in_acc, in_jrk, in_mass, in_time, in_index,
    out_pred, out_acc, out_jrk,
    sources, targets, spread, sums, parts, arrived,
    in_sem, out_sem, src_send, src_recv, tgt_send, tgt_recv, sum_send, sum_recv,
):
    blk, grp = lax.axis_index("blk"), lax.axis_index("grp")
    groups, chunks = active // ROWS, stars // LANES
    power_of_two = n_grp & (n_grp - 1) == 0

    def mate(k):
        return flipped(grp, k) if power_of_two else lax.rem(grp + k, n_grp)

    def back(k):
        return k if power_of_two else n_grp - k

    def ahead(k):
        return lax.rem(blk + k, n_blk)

    barrier = pltpu.get_barrier_semaphore()
    for k in range(1, n_blk):
        pl.semaphore_signal(barrier, inc=1, device_id={"blk": ahead(k)}, device_id_type=pl.DeviceIdType.MESH)
    for k in range(1, n_grp):
        pl.semaphore_signal(barrier, inc=1, device_id={"grp": mate(k)}, device_id_type=pl.DeviceIdType.MESH)

    loads = [
        pltpu.make_async_copy(whole, held, in_sem.at[at])
        for at, (whole, held) in enumerate((
            (position, in_pos), (velocity, in_vel), (accel_old, in_acc), (jerk_old, in_jrk),
            (mass, in_mass), (elapsed, in_time), (index, in_index),
        ))
    ]
    for load in loads:
        load.start()
    for load in loads:
        load.wait()

    step_row = in_time[...]
    half = step_row * step_row * 0.5
    sixth = half * step_row * (1.0 / 3.0)
    new_position = in_pos[...] + step_row * in_vel[...] + half * in_acc[...] + sixth * in_jrk[...]
    new_velocity = in_vel[...] + step_row * in_acc[...] + half * in_jrk[...]
    sources[0, 0:3, :] = new_position
    sources[0, 3:6, :] = new_velocity
    sources[0, 6:7, :] = in_mass[...]
    out_pred[0:3, :] = new_position
    out_pred[3:6, :] = new_velocity

    base = (blk * n_grp + grp) * stars
    offsets = (in_index[...] - base).astype(jnp.float32)
    lane_active = lax.broadcasted_iota(jnp.int32, (ROWS, active), 1)
    row_active = lax.broadcasted_iota(jnp.int32, (ROWS, active), 0)
    lane_stars = lax.broadcasted_iota(jnp.int32, (ROWS, stars), 1)
    lane = lax.broadcasted_iota(jnp.int32, (ROWS, LANES), 1)
    packed = jnp.zeros((ROWS, LANES), jnp.float32)
    for group in range(groups):
        wanted = jnp.sum(jnp.where(lane_active == row_active + group * ROWS, offsets, 0.0), 1, keepdims=True)
        chosen = lane_stars == wanted.astype(jnp.int32)
        for row in range(6):
            value = new_position[row:row + 1] if row < 3 else new_velocity[row - 3:row - 2]
            found = jnp.sum(jnp.where(chosen, value, 0.0), 1, keepdims=True)
            spread[0, group, row] = jnp.broadcast_to(found, (ROWS, LANES))
            packed = jnp.where(lane == group * ROWS + row, found, packed)
    targets[0] = packed

    pl.semaphore_wait(barrier, n_blk - 1 + n_grp - 1)
    near_last = sorted(range(1, n_blk), key=lambda k: -min(k, n_blk - k))
    target_copies = [None] + [
        pltpu.make_async_remote_copy(
            src_ref=targets.at[0], dst_ref=targets.at[back(k)],
            send_sem=tgt_send.at[k], recv_sem=tgt_recv.at[back(k)],
            device_id={"grp": mate(k)}, device_id_type=pl.DeviceIdType.MESH,
        )
        for k in range(1, n_grp)
    ]
    source_copies = [None] + [
        pltpu.make_async_remote_copy(
            src_ref=sources.at[0], dst_ref=sources.at[k],
            send_sem=src_send.at[k], recv_sem=src_recv.at[k],
            device_id={"blk": ahead(k)}, device_id_type=pl.DeviceIdType.MESH,
        )
        for k in range(1, n_blk)
    ]
    for k in near_last:
        source_copies[k].start()
    for k in range(n_grp - 1, 0, -1):
        target_copies[k].start()
    store_pred = pltpu.make_async_copy(out_pred, predicted, out_sem.at[0])
    store_pred.start()

    def pairs(slot, peer, totals):
        totals = list(totals)
        at = [[spread[peer, group, row] for row in range(6)] for group in range(groups)]
        for chunk in range(chunks):
            here = pl.ds(chunk * LANES, LANES)
            star = [jnp.broadcast_to(sources[slot, row:row + 1, here], (ROWS, LANES)) for row in range(7)]
            for group in range(groups):
                me = at[group]
                r = [star[d] - me[d] for d in range(3)]
                u = [star[3 + d] - me[3 + d] for d in range(3)]
                q = (r[0] * r[0] + r[1] * r[1] + r[2] * r[2]) + SOFTENING
                inverse = lax.rsqrt(q)
                square = inverse * inverse
                weight = star[6] * inverse * square
                radial = (r[0] * u[0] + r[1] * u[1] + r[2] * u[2]) * (3.0 * square)
                for d in range(3):
                    spot = group * 6 + d
                    totals[spot] = totals[spot] + weight * r[d]
                    totals[spot + 3] = totals[spot + 3] + weight * (u[d] - radial * r[d])
        return totals

    zeros = [jnp.zeros((ROWS, LANES), jnp.float32)] * (groups * 6)

    def keep(peer, totals):
        for at, value in enumerate(totals):
            sums[peer, at] = value

    def unpack(peer):
        block = targets[peer]
        for group in range(groups):
            for row in range(6):
                at = group * ROWS + row
                spread[peer, group, row] = jnp.broadcast_to(block[:, at:at + 1], (ROWS, LANES))

    order = [0] + near_last[::-1]
    last = order[-1]
    for place, slot in enumerate(order[:-1]):
        if slot:
            source_copies[slot].wait_recv()
        if place == 0:
            keep(0, pairs(slot, 0, zeros))
            for k in range(1, n_grp):
                target_copies[back(k)].wait_recv()

            @pl.loop(1, n_grp)
            def _(peer):
                unpack(peer)
                keep(peer, pairs(slot, peer, zeros))
        else:
            @pl.loop(0, n_grp)
            def _(peer):
                keep(peer, pairs(slot, peer, [sums[peer, at] for at in range(groups * 6)]))

    source_copies[last].wait_recv()
    sum_copies = {}
    for k in list(range(n_grp - 1, 0, -1)) + [0]:
        totals = pairs(last, k, [sums[k, at] for at in range(groups * 6)])
        packed = jnp.zeros((ROWS, LANES), jnp.float32)
        for group in range(groups):
            for row in range(6):
                value = jnp.sum(totals[group * 6 + row], 1, keepdims=True)
                packed = jnp.where(lane == group * ROWS + row, value, packed)
        if k:
            parts[k] = packed
            sum_copies[k] = pltpu.make_async_remote_copy(
                src_ref=parts.at[k], dst_ref=arrived.at[k],
                send_sem=sum_send.at[k], recv_sem=sum_recv.at[k],
                device_id={"grp": mate(k)}, device_id_type=pl.DeviceIdType.MESH,
            )
            sum_copies[k].start()
        else:
            total = packed
    for k in range(1, n_grp):
        sum_copies[k].wait_recv()
        total = total + arrived[k]
    turned = total.T
    for group in range(groups):
        here = pl.ds(group * ROWS, ROWS)
        out_acc[:, here] = turned[group * ROWS:group * ROWS + 3, :]
        out_jrk[:, here] = turned[group * ROWS + 3:group * ROWS + 6, :]
    store_acc = pltpu.make_async_copy(out_acc, accel, out_sem.at[1])
    store_jrk = pltpu.make_async_copy(out_jrk, jerk, out_sem.at[2])
    store_acc.start()
    store_jrk.start()
    for k in range(1, n_blk):
        source_copies[k].wait_send()
    for k in range(1, n_grp):
        target_copies[k].wait_send()
        sum_copies[k].wait_send()
    store_pred.wait()
    store_acc.wait()
    store_jrk.wait()


def local(n_blk, n_grp, position, velocity, accel_old, jerk_old, mass, elapsed, active_index):
    stars, active = position.shape[1], active_index.shape[0]
    groups = active // ROWS
    f32 = jnp.float32
    dma = pltpu.SemaphoreType.DMA
    any_spec = pl.BlockSpec(memory_space=pl.ANY)
    return pl.pallas_call(
        functools.partial(kernel, n_blk, n_grp, stars, active),
        out_shape=(
            jax.ShapeDtypeStruct((6, stars), f32),
            jax.ShapeDtypeStruct((3, active), f32),
            jax.ShapeDtypeStruct((3, active), f32),
        ),
        in_specs=[any_spec] * 7,
        out_specs=(any_spec,) * 3,
        scratch_shapes=[
            pltpu.VMEM((3, stars), f32), pltpu.VMEM((3, stars), f32),
            pltpu.VMEM((3, stars), f32), pltpu.VMEM((3, stars), f32),
            pltpu.VMEM((1, stars), f32), pltpu.VMEM((1, stars), f32),
            pltpu.VMEM((1, active), jnp.int32),
            pltpu.VMEM((6, stars), f32), pltpu.VMEM((3, active), f32), pltpu.VMEM((3, active), f32),
            pltpu.VMEM((n_blk, ROWS, stars), f32),
            pltpu.VMEM((n_grp, ROWS, LANES), f32),
            pltpu.VMEM((n_grp, groups, 6, ROWS, LANES), f32),
            pltpu.VMEM((n_grp, groups * 6, ROWS, LANES), f32),
            pltpu.VMEM((n_grp, ROWS, LANES), f32),
            pltpu.VMEM((n_grp, ROWS, LANES), f32),
            dma((7,)), dma((3,)), dma((n_blk,)), dma((n_blk,)),
            dma((n_grp,)), dma((n_grp,)), dma((n_grp,)), dma((n_grp,)),
        ],
        compiler_params=pltpu.CompilerParams(collective_id=0, has_side_effects=True),
        name="hermite",
    )(
        position, velocity, accel_old, jerk_old,
        mass.reshape(1, stars), elapsed.reshape(1, stars), active_index.reshape(1, active),
    )


def solution(mesh):
    split = P(None, ("blk", "grp"))
    single = P(("blk", "grp"))
    return jax.shard_map(
        functools.partial(local, mesh.shape["blk"], mesh.shape["grp"]),
        mesh=mesh,
        in_specs=(split, split, split, split, single, single, single),
        out_specs=(split, split, split),
        check_vma=False,
    )
```

time: 90.2 us -> 18.5 us (0.21)
  waiting for transfers between devices: 48.9 us -> 0 us
  Pallas kernels: 0 us -> 14.9 us
  between operations: 14.1 us -> 0.65 us
  blocking collectives: 10.6 us -> 0 us
  starting transfers between devices: 6.96 us -> 0 us
  local copies, waits for them, and re-layouts: 6.22 us -> 2.57 us
  other arithmetic: 2.95 us -> 0 us
    unnamed x2 -> x0, waiting for transfers between devices: 32.4 us -> none
    ppermute x8 -> x0, waiting for transfers between devices: 16.5 us -> none  [from_behind(): lax.ppermute(shard, axis, [(i, (i + by) % count) for i in range(count)])]
    pallas_call x0 -> x1, Pallas kernels: none -> 14.9 us  [local(): pl.pallas_call(functools.partial(kernel, n_blk, n_grp, stars, active), ou...]
    all_gather x1 -> x0, blocking collectives: 10.6 us -> none  [local(): group_rows = lax.all_gather(owned_rows, 'grp', axis=1, tiled=True)]
    ppermute x8 -> x0, starting transfers between devices: 6.93 us -> none  [from_behind(): lax.ppermute(shard, axis, [(i, (i + by) % count) for i in range(count)])]
    reduce_sum x8 -> x0, other arithmetic: 2.46 us -> none  [the longest x4 1.6 us: one_block(): accel_part = jnp.sum(weight[None] * separation, 2)]
    unnamed x20 -> x7, local copies, waits for them, and re-layouts: 4.56 us -> 2.57 us
  transfers between devices with their start and end apart: 9 -> 0, of which waited for: 9 -> 0; matrix products, arithmetic and copies ran while one was open for 3% -> 0% of each run, Pallas kernels for 0% -> 0%
where the time goes in v1:
time: 18.5 us; the launch traced here: 18.1 us
  Pallas kernels  14.9 us (81%)
  local copies, waits for them, and re-layouts  2.57 us (14%)
  between operations  0.65 us (4%)
    pallas_call x1, Pallas kernels, local(): pl.pallas_call(functools.partial(kernel, n_blk, n_grp, stars, active), ou...  14.9 us
    unnamed x7, local copies, waits for them, and re-layouts  2.57 us

profile of v1, /device:TPU:0, one launch (start us, length us, event | category | flops | bytes accessed | tf_op | source)
XLA Modules:
  0.0 18.1 jit_solution(18144396110030902228)
XLA Ops:
  0.6 14.9 %hermite.1 = (f32[6,512]{1,0:T(8,128)}, f32[3,16]{1,0:T(4,128)}, f32[3,16]{1,0:T(4,128)}) custom-call(f32[3,512]{1,0:T(4,128)} %position.1, f32[3,512]{1,0:T(4,128)} %velocity.1, f32[3,512]{1,0:T(4,128)} %accel_old.1, f32[3,512]{1,0:T(4,128)} %jerk_old.1, f32[1,512]{1,0:T(1,128)} %bitcast.3, f32[1,512]{1,0:T(1,128)} %bitcast.4, s32[1,16]{1,0:T(1,128)} %bitcast.5), custom_call_target="tpu_custom_call" | custom-call | tf_op jit(solution)/shard_map/hermite/pallas_call | solution.py:217
  15.6 0.0 copy-start.1
  15.6 1.3 %copy.13 = f32[6,512]{1,0:T(8,128)} copy(f32[6,512]{1,0:T(8,128)} %get-tuple-element.6) | data formatting | bytes 24576
  16.9 0.0 copy-done.1
  16.9 0.0 copy-start
  16.9 0.6 %copy.14 = f32[3,16]{1,0:T(4,128)} copy(f32[3,16]{1,0:T(4,128)S(1)} %copy-done.1) | data formatting | bytes 384
  17.5 0.1 copy-done
  17.6 0.6 %copy.15 = f32[3,16]{1,0:T(4,128)} copy(f32[3,16]{1,0:T(4,128)S(1)} %copy-done) | data formatting | bytes 384
Async XLA Ops:
  15.6 1.3 %copy-start.1 = (f32[3,16]{1,0:T(4,128)S(1)}, f32[3,16]{1,0:T(4,128)}, u32[]{:S(2)}) copy-start(f32[3,16]{1,0:T(4,128)} %get-tuple-element.7) | copy-start | bytes 580
  16.9 0.7 %copy-start = (f32[3,16]{1,0:T(4,128)S(1)}, f32[3,16]{1,0:T(4,128)}, u32[]{:S(2)}) copy-start(f32[3,16]{1,0:T(4,128)} %get-tuple-element.8) | copy-start | bytes 580

commit v2 on v1

--- a/solution.py
+++ b/solution.py
@@ -24,11 +24,10 @@
 def kernel(
     n_blk, n_grp, stars, active,
     position, velocity, accel_old, jerk_old, mass, elapsed, index,
-    predicted, accel, jerk,
+    out_pred, out_sum,
     in_pos, in_vel, in_acc, in_jrk, in_mass, in_time, in_index,
-    out_pred, out_acc, out_jrk,
     sources, targets, spread, sums, parts, arrived,
-    in_sem, out_sem, src_send, src_recv, tgt_send, tgt_recv, sum_send, sum_recv,
+    in_sem, src_send, src_recv, tgt_send, tgt_recv, sum_send, sum_recv,
 ):
     blk, grp = lax.axis_index("blk"), lax.axis_index("grp")
     groups, chunks = active // ROWS, stars // LANES
@@ -42,12 +41,6 @@
 
     def ahead(k):
         return lax.rem(blk + k, n_blk)
-
-    barrier = pltpu.get_barrier_semaphore()
-    for k in range(1, n_blk):
-        pl.semaphore_signal(barrier, inc=1, device_id={"blk": ahead(k)}, device_id_type=pl.DeviceIdType.MESH)
-    for k in range(1, n_grp):
-        pl.semaphore_signal(barrier, inc=1, device_id={"grp": mate(k)}, device_id_type=pl.DeviceIdType.MESH)
 
     loads = [
         pltpu.make_async_copy(whole, held, in_sem.at[at])
@@ -58,7 +51,23 @@
     ]
     for load in loads:
         load.start()
-    for load in loads:
+
+    barrier = pltpu.get_barrier_semaphore()
+    for k in range(1, n_blk):
+        pl.semaphore_signal(barrier, inc=1, device_id={"blk": ahead(k)}, device_id_type=pl.DeviceIdType.MESH)
+    for k in range(1, n_grp):
+        pl.semaphore_signal(barrier, inc=1, device_id={"grp": mate(k)}, device_id_type=pl.DeviceIdType.MESH)
+
+    loads[-1].wait()
+    base = (blk * n_grp + grp) * stars
+    offsets = (in_index[...] - base).astype(jnp.float32)
+    lane_active = lax.broadcasted_iota(jnp.int32, (ROWS, active), 1)
+    row_active = lax.broadcasted_iota(jnp.int32, (ROWS, active), 0)
+    wanted = [
+        jnp.sum(jnp.where(lane_active == row_active + group * ROWS, offsets, 0.0), 1, keepdims=True)
+        for group in range(groups)
+    ]
+    for load in loads[:-1]:
         load.wait()
 
     step_row = in_time[...]
@@ -72,23 +81,6 @@
     out_pred[0:3, :] = new_position
     out_pred[3:6, :] = new_velocity
 
-    base = (blk * n_grp + grp) * stars
-    offsets = (in_index[...] - base).astype(jnp.float32)
-    lane_active = lax.broadcasted_iota(jnp.int32, (ROWS, active), 1)
-    row_active = lax.broadcasted_iota(jnp.int32, (ROWS, active), 0)
-    lane_stars = lax.broadcasted_iota(jnp.int32, (ROWS, stars), 1)
-    lane = lax.broadcasted_iota(jnp.int32, (ROWS, LANES), 1)
-    packed = jnp.zeros((ROWS, LANES), jnp.float32)
-    for group in range(groups):
-        wanted = jnp.sum(jnp.where(lane_active == row_active + group * ROWS, offsets, 0.0), 1, keepdims=True)
-        chosen = lane_stars == wanted.astype(jnp.int32)
-        for row in range(6):
-            value = new_position[row:row + 1] if row < 3 else new_velocity[row - 3:row - 2]
-            found = jnp.sum(jnp.where(chosen, value, 0.0), 1, keepdims=True)
-            spread[0, group, row] = jnp.broadcast_to(found, (ROWS, LANES))
-            packed = jnp.where(lane == group * ROWS + row, found, packed)
-    targets[0] = packed
-
     pl.semaphore_wait(barrier, n_blk - 1 + n_grp - 1)
     near_last = sorted(range(1, n_blk), key=lambda k: -min(k, n_blk - k))
     target_copies = [None] + [
@@ -109,10 +101,20 @@
     ]
     for k in near_last:
         source_copies[k].start()
+
+    lane_stars = lax.broadcasted_iota(jnp.int32, (ROWS, stars), 1)
+    lane = lax.broadcasted_iota(jnp.int32, (ROWS, LANES), 1)
+    packed = jnp.zeros((ROWS, LANES), jnp.float32)
+    for group in range(groups):
+        chosen = lane_stars == wanted[group].astype(jnp.int32)
+        for row in range(6):
+            value = new_position[row:row + 1] if row < 3 else new_velocity[row - 3:row - 2]
+            found = jnp.sum(jnp.where(chosen, value, 0.0), 1, keepdims=True)
+            spread[0, group, row] = jnp.broadcast_to(found, (ROWS, LANES))
+            packed = jnp.where(lane == group * ROWS + row, found, packed)
+    targets[0] = packed
     for k in range(n_grp - 1, 0, -1):
         target_copies[k].start()
-    store_pred = pltpu.make_async_copy(out_pred, predicted, out_sem.at[0])
-    store_pred.start()
 
     def pairs(slot, peer, totals):
         totals = list(totals)
@@ -189,20 +191,26 @@
     for k in range(1, n_grp):
         sum_copies[k].wait_recv()
         total = total + arrived[k]
-    turned = total.T
-    for group in range(groups):
-        here = pl.ds(group * ROWS, ROWS)
-        out_acc[:, here] = turned[group * ROWS:group * ROWS + 3, :]
-        out_jrk[:, here] = turned[group * ROWS + 3:group * ROWS + 6, :]
-    store_acc = pltpu.make_async_copy(out_acc, accel, out_sem.at[1])
-    store_jrk = pltpu.make_async_copy(out_jrk, jerk, out_sem.at[2])
-    store_acc.start()
-    store_jrk.start()
+    out_sum[...] = total
     for k in range(1, n_blk):
         source_copies[k].wait_send()
     for k in range(1, n_grp):
         target_copies[k].wait_send()
         sum_copies[k].wait_send()
+
+
+def finish(groups, held, total, predicted, accel, jerk, out_acc, out_jrk, sem):
+    store_pred = pltpu.make_async_copy(held, predicted, sem.at[0])
+    store_pred.start()
+    turned = total[...].T
+    for group in range(groups):
+        here = pl.ds(group * ROWS, ROWS)
+        out_acc[:, here] = turned[group * ROWS:group * ROWS + 3, :]
+        out_jrk[:, here] = turned[group * ROWS + 3:group * ROWS + 6, :]
+    store_acc = pltpu.make_async_copy(out_acc, accel, sem.at[1])
+    store_jrk = pltpu.make_async_copy(out_jrk, jerk, sem.at[2])
+    store_acc.start()
+    store_jrk.start()
     store_pred.wait()
     store_acc.wait()
     store_jrk.wait()
@@ -213,37 +221,48 @@
     groups = active // ROWS
     f32 = jnp.float32
     dma = pltpu.SemaphoreType.DMA
-    any_spec = pl.BlockSpec(memory_space=pl.ANY)
-    return pl.pallas_call(
+    hbm_spec = pl.BlockSpec(memory_space=pltpu.HBM)
+    vmem_spec = pl.BlockSpec(memory_space=pltpu.VMEM)
+    held, total = pl.pallas_call(
         functools.partial(kernel, n_blk, n_grp, stars, active),
-        out_shape=(
-            jax.ShapeDtypeStruct((6, stars), f32),
-            jax.ShapeDtypeStruct((3, active), f32),
-            jax.ShapeDtypeStruct((3, active), f32),
-        ),
-        in_specs=[any_spec] * 7,
-        out_specs=(any_spec,) * 3,
+        out_shape=(pltpu.VMEM((6, stars), f32), pltpu.VMEM((ROWS, LANES), f32)),
+        in_specs=[hbm_spec] * 7,
+        out_specs=(vmem_spec,) * 2,
         scratch_shapes=[
             pltpu.VMEM((3, stars), f32), pltpu.VMEM((3, stars), f32),
             pltpu.VMEM((3, stars), f32), pltpu.VMEM((3, stars), f32),
             pltpu.VMEM((1, stars), f32), pltpu.VMEM((1, stars), f32),
             pltpu.VMEM((1, active), jnp.int32),
-            pltpu.VMEM((6, stars), f32), pltpu.VMEM((3, active), f32), pltpu.VMEM((3, active), f32),
             pltpu.VMEM((n_blk, ROWS, stars), f32),
             pltpu.VMEM((n_grp, ROWS, LANES), f32),
             pltpu.VMEM((n_grp, groups, 6, ROWS, LANES), f32),
             pltpu.VMEM((n_grp, groups * 6, ROWS, LANES), f32),
             pltpu.VMEM((n_grp, ROWS, LANES), f32),
             pltpu.VMEM((n_grp, ROWS, LANES), f32),
-            dma((7,)), dma((3,)), dma((n_blk,)), dma((n_blk,)),
+            dma((7,)), dma((n_blk,)), dma((n_blk,)),
             dma((n_grp,)), dma((n_grp,)), dma((n_grp,)), dma((n_grp,)),
         ],
-        compiler_params=pltpu.CompilerParams(collective_id=0, has_side_effects=True),
+        compiler_params=pltpu.CompilerParams(
+            collective_id=0, has_side_effects=True,
+        ),
         name="hermite",
     )(
         position, velocity, accel_old, jerk_old,
         mass.reshape(1, stars), elapsed.reshape(1, stars), active_index.reshape(1, active),
     )
+    return pl.pallas_call(
+        functools.partial(finish, groups),
+        out_shape=(
+            jax.ShapeDtypeStruct((6, stars), f32),
+            jax.ShapeDtypeStruct((3, active), f32),
+            jax.ShapeDtypeStruct((3, active), f32),
+        ),
+        in_specs=[vmem_spec] * 2,
+        out_specs=(hbm_spec,) * 3,
+        scratch_shapes=[pltpu.VMEM((3, active), f32), pltpu.VMEM((3, active), f32), dma((3,))],
+        compiler_params=pltpu.CompilerParams(vmem_limit_bytes=16 * 1024 * 1024),
+        name="finish",
+    )(held, total)
 
 
 def solution(mesh):

time: 18.5 us -> 15.9 us (0.86)
  local copies, waits for them, and re-layouts: 2.57 us -> 0 us
  Pallas kernels: 14.9 us -> 15.1 us
    unnamed x7 -> x0, local copies, waits for them, and re-layouts: 2.57 us -> none
    pallas_call x0 -> x1, Pallas kernels: none -> 0.73 us  [local(): pl.pallas_call(functools.partial(finish, groups), out_shape=(jax.ShapeDty...]
    pallas_call x1, Pallas kernels: 14.9 us -> 14.3 us  [local(): pl.pallas_call(functools.partial(kernel, n_blk, n_grp, stars, active), ou...]
where the time goes in v2:
time: 15.9 us; the launch traced here: 15.7 us
  Pallas kernels  15.1 us (95%)
  between operations  0.64 us (4%)
    pallas_call x1, Pallas kernels, local(): pl.pallas_call(functools.partial(kernel, n_blk, n_grp, stars, active), ou...  14.3 us
    pallas_call x1, Pallas kernels, local(): pl.pallas_call(functools.partial(finish, groups), out_shape=(jax.ShapeDty...  0.73 us

profile of v2, /device:TPU:0, one launch (start us, length us, event | category | flops | bytes accessed | tf_op | source)
XLA Modules:
  0.0 15.7 jit_solution(17437216903068240160)
XLA Ops:
  0.6 14.3 %hermite.1 = (f32[6,512]{1,0:T(8,128)S(1)}, f32[8,128]{1,0:T(8,128)S(1)}) custom-call(f32[3,512]{1,0:T(4,128)} %position.1, f32[3,512]{1,0:T(4,128)} %velocity.1, f32[3,512]{1,0:T(4,128)} %accel_old.1, f32[3,512]{1,0:T(4,128)} %jerk_old.1, f32[1,512]{1,0:T(1,128)} %bitcast.3, f32[1,512]{1,0:T(1,128)} %bitcast.4, s32[1,16]{1,0:T(1,128)} %bitcast.5), custom_call_target="tpu_custom_call" | custom-call | tf_op jit(solution)/shard_map/hermite/pallas_call | solution.py:226
  15.0 0.7 %finish.1 = (f32[6,512]{1,0:T(8,128)}, f32[3,16]{1,0:T(4,128)}, f32[3,16]{1,0:T(4,128)}) custom-call(f32[6,512]{1,0:T(8,128)S(1)} %get-tuple-element.5.held, f32[8,128]{1,0:T(8,128)S(1)} %get-tuple-element.6.total), custom_call_target="tpu_custom_call" | custom-call | tf_op jit(solution)/shard_map/finish/pallas_call | solution.py:253

commit v3 on v2

--- a/solution.py
+++ b/solution.py
@@ -82,7 +82,8 @@
     out_pred[3:6, :] = new_velocity
 
     pl.semaphore_wait(barrier, n_blk - 1 + n_grp - 1)
-    near_last = sorted(range(1, n_blk), key=lambda k: -min(k, n_blk - k))
+    order = [0] + sorted(range(1, n_blk), key=lambda k: min(k, n_blk - k))
+    last = n_blk - 1
     target_copies = [None] + [
         pltpu.make_async_remote_copy(
             src_ref=targets.at[0], dst_ref=targets.at[back(k)],
@@ -93,13 +94,13 @@
     ]
     source_copies = [None] + [
         pltpu.make_async_remote_copy(
-            src_ref=sources.at[0], dst_ref=sources.at[k],
+            src_ref=sources.at[0], dst_ref=sources.at[order.index(k)],
             send_sem=src_send.at[k], recv_sem=src_recv.at[k],
             device_id={"blk": ahead(k)}, device_id_type=pl.DeviceIdType.MESH,
         )
         for k in range(1, n_blk)
     ]
-    for k in near_last:
+    for k in order[:0:-1]:
         source_copies[k].start()
 
     lane_stars = lax.broadcasted_iota(jnp.int32, (ROWS, stars), 1)
@@ -137,57 +138,62 @@
                     totals[spot + 3] = totals[spot + 3] + weight * (u[d] - radial * r[d])
         return totals
 
-    zeros = [jnp.zeros((ROWS, LANES), jnp.float32)] * (groups * 6)
+    zeros = (jnp.zeros((ROWS, LANES), jnp.float32),) * (groups * 6)
+
+    def over(first, end, peer, totals):
+        return lax.fori_loop(first, end, lambda place, held: tuple(pairs(place, peer, held)), tuple(totals))
 
     def keep(peer, totals):
         for at, value in enumerate(totals):
             sums[peer, at] = value
 
+    def kept(peer):
+        return tuple(sums[peer, at] for at in range(groups * 6))
+
     def unpack(peer):
+        target_copies[back(peer)].wait_recv()
         block = targets[peer]
         for group in range(groups):
             for row in range(6):
                 at = group * ROWS + row
                 spread[peer, group, row] = jnp.broadcast_to(block[:, at:at + 1], (ROWS, LANES))
 
-    order = [0] + near_last[::-1]
-    last = order[-1]
-    for place, slot in enumerate(order[:-1]):
-        if slot:
-            source_copies[slot].wait_recv()
-        if place == 0:
-            keep(0, pairs(slot, 0, zeros))
-            for k in range(1, n_grp):
-                target_copies[back(k)].wait_recv()
-
-            @pl.loop(1, n_grp)
-            def _(peer):
-                unpack(peer)
-                keep(peer, pairs(slot, peer, zeros))
-        else:
-            @pl.loop(0, n_grp)
-            def _(peer):
-                keep(peer, pairs(slot, peer, [sums[peer, at] for at in range(groups * 6)]))
-
-    source_copies[last].wait_recv()
-    sum_copies = {}
-    for k in list(range(n_grp - 1, 0, -1)) + [0]:
-        totals = pairs(last, k, [sums[k, at] for at in range(groups * 6)])
+    def pack(totals):
         packed = jnp.zeros((ROWS, LANES), jnp.float32)
         for group in range(groups):
             for row in range(6):
                 value = jnp.sum(totals[group * 6 + row], 1, keepdims=True)
                 packed = jnp.where(lane == group * ROWS + row, value, packed)
-        if k:
-            parts[k] = packed
-            sum_copies[k] = pltpu.make_async_remote_copy(
-                src_ref=parts.at[k], dst_ref=arrived.at[k],
-                send_sem=sum_send.at[k], recv_sem=sum_recv.at[k],
-                device_id={"grp": mate(k)}, device_id_type=pl.DeviceIdType.MESH,
-            )
-            sum_copies[k].start()
-        else:
-            total = packed
+        return packed
+
+    sum_copies = {}
+
+    def send(k, totals):
+        parts[k] = pack(totals)
+        sum_copies[k] = pltpu.make_async_remote_copy(
+            src_ref=parts.at[k], dst_ref=arrived.at[k],
+            send_sem=sum_send.at[k], recv_sem=sum_recv.at[k],
+            device_id={"grp": mate(k)}, device_id_type=pl.DeviceIdType.MESH,
+        )
+        sum_copies[k].start()
+
+    far = list(range(n_grp - 1, 0, -1))
+    lead = max(1, n_grp // 4)
+    totals = over(0, 1, 0, zeros)
+    for k in order[1:-1]:
+        source_copies[k].wait_recv()
+    keep(0, over(1, last, 0, totals))
+    for k in far[:lead]:
+        unpack(k)
+        keep(k, over(0, last, k, zeros))
+    if last:
+        source_copies[order[last]].wait_recv()
+    for k in far[:lead]:
+        send(k, over(last, n_blk, k, kept(k)))
+    for k in far[lead:]:
+        unpack(k)
+        send(k, over(0, n_blk, k, zeros))
+    total = pack(over(last, n_blk, 0, kept(0)))
     for k in range(1, n_grp):
         sum_copies[k].wait_recv()
         total = total + arrived[k]

time: 15.9 us -> 16.1 us (1.013)
  Pallas kernels: 15.1 us -> 15.3 us
    pallas_call x1, Pallas kernels: 14.3 us -> 14.6 us  [local(): pl.pallas_call(functools.partial(kernel, n_blk, n_grp, stars, active), ou...]
where the time goes in v3:
time: 16.1 us; the launch traced here: 16 us
  Pallas kernels  15.3 us (95%)
  between operations  0.64 us (4%)
    pallas_call x1, Pallas kernels, local(): pl.pallas_call(functools.partial(kernel, n_blk, n_grp, stars, active), ou...  14.6 us
    pallas_call x1, Pallas kernels, local(): pl.pallas_call(functools.partial(finish, groups), out_shape=(jax.ShapeDty...  0.73 us

profile of v3, /device:TPU:0, one launch (start us, length us, event | category | flops | bytes accessed | tf_op | source)
XLA Modules:
  0.0 16.0 jit_solution(10271088982688419561)
XLA Ops:
  0.6 14.6 %hermite.1 = (f32[6,512]{1,0:T(8,128)S(1)}, f32[8,128]{1,0:T(8,128)S(1)}) custom-call(f32[3,512]{1,0:T(4,128)} %position.1, f32[3,512]{1,0:T(4,128)} %velocity.1, f32[3,512]{1,0:T(4,128)} %accel_old.1, f32[3,512]{1,0:T(4,128)} %jerk_old.1, f32[1,512]{1,0:T(1,128)} %bitcast.3, f32[1,512]{1,0:T(1,128)} %bitcast.4, s32[1,16]{1,0:T(1,128)} %bitcast.5), custom_call_target="tpu_custom_call" | custom-call | tf_op jit(solution)/shard_map/hermite/pallas_call | solution.py:232
  15.2 0.7 %finish.1 = (f32[6,512]{1,0:T(8,128)}, f32[3,16]{1,0:T(4,128)}, f32[3,16]{1,0:T(4,128)}) custom-call(f32[6,512]{1,0:T(8,128)S(1)} %get-tuple-element.5.held, f32[8,128]{1,0:T(8,128)S(1)} %get-tuple-element.6.total), custom_call_target="tpu_custom_call" | custom-call | tf_op jit(solution)/shard_map/finish/pallas_call | solution.py:259

commit v4 on v3

--- a/solution.py
+++ b/solution.py
@@ -141,7 +141,7 @@
     zeros = (jnp.zeros((ROWS, LANES), jnp.float32),) * (groups * 6)
 
     def over(first, end, peer, totals):
-        return lax.fori_loop(first, end, lambda place, held: tuple(pairs(place, peer, held)), tuple(totals))
+        return lax.fori_loop(first, end, lambda place, held: tuple(pairs(place, peer, held)), tuple(totals), unroll=end - first <= 4)
 
     def keep(peer, totals):
         for at, value in enumerate(totals):
@@ -178,22 +178,15 @@
         sum_copies[k].start()
 
     far = list(range(n_grp - 1, 0, -1))
-    lead = max(1, n_grp // 4)
-    totals = over(0, 1, 0, zeros)
-    for k in order[1:-1]:
+    keep(0, over(0, 1, 0, zeros))
+    for k in far:
+        unpack(k)
+        keep(k, over(0, 1, k, zeros))
+    for k in order[1:]:
         source_copies[k].wait_recv()
-    keep(0, over(1, last, 0, totals))
-    for k in far[:lead]:
-        unpack(k)
-        keep(k, over(0, last, k, zeros))
-    if last:
-        source_copies[order[last]].wait_recv()
-    for k in far[:lead]:
-        send(k, over(last, n_blk, k, kept(k)))
-    for k in far[lead:]:
-        unpack(k)
-        send(k, over(0, n_blk, k, zeros))
-    total = pack(over(last, n_blk, 0, kept(0)))
+    for k in far:
+        send(k, over(1, n_blk, k, kept(k)))
+    total = pack(over(1, n_blk, 0, kept(0)))
     for k in range(1, n_grp):
         sum_copies[k].wait_recv()
         total = total + arrived[k]

time: 16.1 us -> 15.4 us (0.957)
  Pallas kernels: 15.3 us -> 14.6 us
    pallas_call x1, Pallas kernels: 14.6 us -> 13.9 us  [local(): pl.pallas_call(functools.partial(kernel, n_blk, n_grp, stars, active), ou...]
where the time goes in v4:
time: 15.4 us; the launch traced here: 15.2 us
  Pallas kernels  14.6 us (95%)
  between operations  0.64 us (4%)
    pallas_call x1, Pallas kernels, local(): pl.pallas_call(functools.partial(kernel, n_blk, n_grp, stars, active), ou...  13.9 us
    pallas_call x1, Pallas kernels, local(): pl.pallas_call(functools.partial(finish, groups), out_shape=(jax.ShapeDty...  0.73 us

profile of v4, /device:TPU:0, one launch (start us, length us, event | category | flops | bytes accessed | tf_op | source)
XLA Modules:
  0.0 15.2 jit_solution(15449927987894368685)
XLA Ops:
  0.6 13.9 %hermite.1 = (f32[6,512]{1,0:T(8,128)S(1)}, f32[8,128]{1,0:T(8,128)S(1)}) custom-call(f32[3,512]{1,0:T(4,128)} %position.1, f32[3,512]{1,0:T(4,128)} %velocity.1, f32[3,512]{1,0:T(4,128)} %accel_old.1, f32[3,512]{1,0:T(4,128)} %jerk_old.1, f32[1,512]{1,0:T(1,128)} %bitcast.3, f32[1,512]{1,0:T(1,128)} %bitcast.4, s32[1,16]{1,0:T(1,128)} %bitcast.5), custom_call_target="tpu_custom_call" | custom-call | tf_op jit(solution)/shard_map/hermite/pallas_call | solution.py:225
  14.5 0.7 %finish.1 = (f32[6,512]{1,0:T(8,128)}, f32[3,16]{1,0:T(4,128)}, f32[3,16]{1,0:T(4,128)}) custom-call(f32[6,512]{1,0:T(8,128)S(1)} %get-tuple-element.5.held, f32[8,128]{1,0:T(8,128)S(1)} %get-tuple-element.6.total), custom_call_target="tpu_custom_call" | custom-call | tf_op jit(solution)/shard_map/finish/pallas_call | solution.py:252
